TPU v7x, 32 devices: a whole 2x2x4 slice. The times are simulated.
32 devices in a mesh: dp: 8 (over z, y), tensor: 4 (over x, core).
Axes of the slice: x: 2, y: 2, z: 4, core: 2. Of those that a mesh axis runs over, the one named last changes fastest.
Arguments:
- tokens: bfloat16 [12288, 768], P('dp'), may hold values from -6 to 6
- segment_ids: int32 [24, 512], P('dp'), may hold values from 0 to 16, as said below
- prev_scores: bfloat16 [24, 12, 512, 512], P('dp', 'tensor'), may hold values from -6 to 6
- out_grad: bfloat16 [12288, 768], P('dp'), may hold values from -6 to 6
- attn_in_master: float32 [3, 768, 768], P(None, 'dp', 'tensor'), may hold values from -0.21875 to 0.21875
- attn_out_master: float32 [768, 768], P('tensor', 'dp'), may hold values from -0.875 to 0.875
- ffn_in_master: float32 [768, 3072], P('dp', 'tensor'), may hold values from -0.21875 to 0.21875
- ffn_out_master: float32 [3072, 768], P('tensor', 'dp'), may hold values from -0.109375 to 0.109375
- attn_in_first: float32 [3, 768, 768], P(None, 'dp', 'tensor'), may hold values from -0.0024414062 to 0.0024414062
- attn_out_first: float32 [768, 768], P('tensor', 'dp'), may hold values from -0.0024414062 to 0.0024414062
- ffn_in_first: float32 [768, 3072], P('dp', 'tensor'), may hold values from -0.0024414062 to 0.0024414062
- ffn_out_first: float32 [3072, 768], P('tensor', 'dp'), may hold values from -0.0024414062 to 0.0024414062
- attn_in_second: float32 [3, 768, 768], P(None, 'dp', 'tensor'), may hold values from 1.4110135e-07 to 5.644054e-07
- attn_out_second: float32 [768, 768], P('tensor', 'dp'), may hold values from 1.4110135e-07 to 5.644054e-07
- ffn_in_second: float32 [768, 3072], P('dp', 'tensor'), may hold values from 1.4110135e-07 to 5.644054e-07
- ffn_out_second: float32 [3072, 768], P('tensor', 'dp'), may hold values from 1.4110135e-07 to 5.644054e-07
- qv_bias: float32 [2, 768], P(None, 'tensor'), may hold values from -1.75 to 1.75
- ffn_bias: float32 [3072], P('tensor'), may hold values from -1.75 to 1.75
- row_params: float32 [6, 768], replicated, may hold values from -0.75 to 1.65, as said below
- qv_bias_first: float32 [2, 768], P(None, 'tensor'), may hold values from -0.009765625 to 0.009765625
- ffn_bias_first: float32 [3072], P('tensor'), may hold values from -0.0024414062 to 0.0024414062
- row_params_first: float32 [6, 768], replicated, may hold values from -0.009765625 to 0.009765625
- qv_bias_second: float32 [2, 768], P(None, 'tensor'), may hold values from 2.2576216e-06 to 9.030487e-06
- ffn_bias_second: float32 [3072], P('tensor'), may hold values from 7.0550676e-08 to 2.822027e-07
- row_params_second: float32 [6, 768], replicated, may hold values from 2.2576216e-06 to 9.030487e-06
Outputs:
- out_tokens: bfloat16 [12288, 768], P('dp')
- tokens_grad: float32 [12288, 768], P('dp')
- scores_grad: float32 [24, 12, 512, 512], P('dp', 'tensor')
- grad_norm: float32 [], replicated
- attn_in_new: float32 [3, 768, 768], P(None, 'dp', 'tensor')
- attn_out_new: float32 [768, 768], P('tensor', 'dp')
- ffn_in_new: float32 [768, 3072], P('dp', 'tensor')
- ffn_out_new: float32 [3072, 768], P('tensor', 'dp')
- attn_in_first_new: float32 [3, 768, 768], P(None, 'dp', 'tensor')
- attn_out_first_new: float32 [768, 768], P('tensor', 'dp')
- ffn_in_first_new: float32 [768, 3072], P('dp', 'tensor')
- ffn_out_first_new: float32 [3072, 768], P('tensor', 'dp')
- attn_in_second_new: float32 [3, 768, 768], P(None, 'dp', 'tensor')
- attn_out_second_new: float32 [768, 768], P('tensor', 'dp')
- ffn_in_second_new: float32 [768, 3072], P('dp', 'tensor')
- ffn_out_second_new: float32 [3072, 768], P('tensor', 'dp')
- attn_in_copy: bfloat16 [3, 768, 768], P(None, 'dp', 'tensor')
- attn_out_copy: bfloat16 [768, 768], P('tensor', 'dp')
- ffn_in_copy: bfloat16 [768, 3072], P('dp', 'tensor')
- ffn_out_copy: bfloat16 [3072, 768], P('tensor', 'dp')
- qv_bias_new: float32 [2, 768], P(None, 'tensor')
- ffn_bias_new: float32 [3072], P('tensor')
- row_params_new: float32 [6, 768], replicated
- qv_bias_first_new: float32 [2, 768], P(None, 'tensor')
- ffn_bias_first_new: float32 [3072], P('tensor')
- row_params_first_new: float32 [6, 768], replicated
- qv_bias_second_new: float32 [2, 768], P(None, 'tensor')
- ffn_bias_second_new: float32 [3072], P('tensor')
- row_params_second_new: float32 [6, 768], replicated
Inputs may be any that keep to these rules, and one draw needn't show every extreme that they name: `segment_ids`: in each pack, live slots come first and empty slots (0) last; live ids start at 1 and rise by one from one sequence to the next; sequences start at multiples of 32 slots; a pack holds 128, 256, 384 or 512 live slots; the first pack holds one sequence of 512 slots, the second pack 3 * 128 live slots, the last pack 16 sequences of 32 slots. `row_params`: rows 0 and 1 lie between 0.35 and 1.65.
All inputs are finite; a program needn't handle non-finite values.
Results may differ from a plain program's by a relative error of at most 0.012.
The roundings to bfloat16 on the way count: a program that leaves them out, or rounds other values in their place, can miss the bound.
Values may be sent and summed in bfloat16 or wider, within the bound.
A program may use at most 128 MiB of HBM per device.

v0:
```python
from functools import partial
import jax
import jax.numpy as jnp
from jax import lax
from jax.sharding import PartitionSpec as P

D = 768
STEP = 5
beta_one = 0.5
beta_two = 0.5
weight_decay = 0.01
adam_eps = 1e-08
norm_eps = 1e-06
small_rate = 0.5


def layer_norm(rows_in, gain_row, shift_row):
    row_mean = jnp.mean(rows_in, axis=-1, keepdims=True)
    centred = rows_in - row_mean
    spread = jnp.mean(centred * centred, axis=-1, keepdims=True)
    return centred * lax.rsqrt(spread + norm_eps) * gain_row + shift_row


def masked_scores(scale, query_heads, key_heads, prev_block, seg_ids):
    same_seq = seg_ids[:, None] == seg_ids[None, :]
    scores = jnp.einsum(
        "qhe,khe->hqk", query_heads, key_heads, preferred_element_type=jnp.float32
    ) * scale + prev_block.astype(jnp.float32)
    return jnp.where(same_seq[None], scores, -1000000000.0)


def attend(scale, pieces):
    query_heads, key_heads, value_heads, prev_block, seg_ids = pieces
    scores = masked_scores(scale, query_heads, key_heads, prev_block, seg_ids)
    row_top = jnp.max(scores, axis=-1, keepdims=True)
    expo = jnp.exp(scores - row_top)
    row_total = jnp.sum(expo, axis=-1, keepdims=True)
    weights_low = (expo / row_total).astype(jnp.bfloat16)
    context_heads = jnp.einsum(
        "hqk,khe->qhe", weights_low, value_heads, preferred_element_type=jnp.float32
    )
    return (context_heads.astype(jnp.bfloat16), row_top + jnp.log(row_total))


def attend_back(scale, pieces):
    query_heads, key_heads, value_heads, prev_block, seg_ids, row_lse, grad_heads = pieces
    scores = masked_scores(scale, query_heads, key_heads, prev_block, seg_ids)
    soft = jnp.exp(scores - row_lse)
    soft_low = soft.astype(jnp.bfloat16)
    grad_soft = jnp.einsum(
        "qhe,khe->hqk", grad_heads, value_heads, preferred_element_type=jnp.float32
    )
    row_dot = jnp.sum(soft * grad_soft, axis=-1, keepdims=True)
    score_grad = (soft * (grad_soft - row_dot)).astype(jnp.bfloat16)
    grad_query = (
        jnp.einsum("hqk,khe->qhe", score_grad, key_heads, preferred_element_type=jnp.float32)
        * scale
    ).astype(jnp.bfloat16)
    grad_key = (
        jnp.einsum("hqk,qhe->khe", score_grad, query_heads, preferred_element_type=jnp.float32)
        * scale
    ).astype(jnp.bfloat16)
    grad_value = jnp.einsum(
        "hqk,qhe->khe", soft_low, grad_heads, preferred_element_type=jnp.float32
    ).astype(jnp.bfloat16)
    return (grad_query, grad_key, grad_value, score_grad.astype(jnp.float32))


def adam_update(weight, gradient, first_moment, second_moment, decay_rate, learn_rate):
    first_new = beta_one * first_moment + (1.0 - beta_one) * gradient
    second_new = beta_two * second_moment + (1.0 - beta_two) * gradient * gradient
    corrected = (
        first_new
        / (1.0 - beta_one**STEP)
        / (jnp.sqrt(second_new / (1.0 - beta_two**STEP)) + adam_eps)
    )
    return (weight - learn_rate * (corrected + decay_rate * weight), first_new, second_new)


def on_device(
    tokens,
    segment_ids,
    prev_scores,
    out_grad,
    attn_in_master,
    attn_out_master,
    ffn_in_master,
    ffn_out_master,
    attn_in_first,
    attn_out_first,
    ffn_in_first,
    ffn_out_first,
    attn_in_second,
    attn_out_second,
    ffn_in_second,
    ffn_out_second,
    qv_bias,
    ffn_bias,
    row_params,
    qv_bias_first,
    ffn_bias_first,
    row_params_first,
    qv_bias_second,
    ffn_bias_second,
    row_params_second,
):
    attn_in, attn_out, ffn_in, ffn_out = (
        lax.all_gather(attn_in_master.astype(jnp.bfloat16), "dp", axis=1, tiled=True),
        lax.all_gather(attn_out_master.astype(jnp.bfloat16), "dp", axis=1, tiled=True),
        lax.all_gather(ffn_in_master.astype(jnp.bfloat16), "dp", axis=0, tiled=True),
        lax.all_gather(ffn_out_master.astype(jnp.bfloat16), "dp", axis=1, tiled=True),
    )
    pack_count, pack_len = segment_ids.shape
    head_count = prev_scores.shape[1]
    head_width = attn_in.shape[2] // head_count
    scale = head_width ** (-0.5)
    token_count = tokens.shape[0]
    dp_count = lax.axis_size("dp")
    tensor_count = lax.axis_size("tensor")

    def split_heads(matrix):
        return matrix.reshape(pack_count, pack_len, head_count, head_width)

    projected = jnp.einsum("td,cde->cte", tokens, attn_in, preferred_element_type=jnp.float32)
    query_rows = (projected[0] + qv_bias[0]).astype(jnp.bfloat16)
    key_rows = projected[1].astype(jnp.bfloat16)
    value_rows = (projected[2] + qv_bias[1]).astype(jnp.bfloat16)
    query_heads = split_heads(query_rows)
    key_heads = split_heads(key_rows)
    value_heads = split_heads(value_rows)
    context_heads, row_lse = lax.map(
        partial(attend, scale), (query_heads, key_heads, value_heads, prev_scores, segment_ids)
    )
    context = context_heads.reshape(token_count, -1)
    attn_partial = jnp.dot(context, attn_out, preferred_element_type=jnp.float32)
    live_whole = (segment_ids > 0).astype(jnp.float32).reshape(token_count, 1)
    rows_start = tokens.astype(jnp.float32)
    attended = lax.psum(attn_partial, "tensor") + row_params[2]
    cotangent = out_grad.astype(jnp.float32)
    residual_one = rows_start + attended
    normed, first_pull = jax.vjp(layer_norm, residual_one, row_params[0], row_params[3])
    normed_low = normed.astype(jnp.bfloat16)
    pre_act = jnp.dot(normed_low, ffn_in, preferred_element_type=jnp.float32) + ffn_bias
    activation, gelu_pull = jax.vjp(partial(jax.nn.gelu, approximate=False), pre_act)
    act_low = activation.astype(jnp.bfloat16)
    ffn_partial = jnp.dot(act_low, ffn_out, preferred_element_type=jnp.float32)
    ffn_output = lax.psum(ffn_partial, "tensor") + row_params[4]

    def final_norm(rows_in, gain_row, shift_row):
        return layer_norm(rows_in, gain_row, shift_row) * live_whole

    final_rows, second_pull = jax.vjp(final_norm, normed + ffn_output, row_params[1], row_params[5])
    final_low = final_rows.astype(jnp.bfloat16)
    grad_res_two, grad_gain_two, grad_shift_two = second_pull(cotangent)
    grad_ffn_low = grad_res_two.astype(jnp.bfloat16)
    grad_ffn_out_bias = jnp.sum(grad_ffn_low.astype(jnp.float32), axis=0)
    grad_ffn_out = jnp.einsum(
        "tf,td->fd", act_low, grad_ffn_low, preferred_element_type=jnp.float32
    )
    grad_act = jnp.einsum("td,fd->tf", grad_ffn_low, ffn_out, preferred_element_type=jnp.float32)
    (grad_pre,) = gelu_pull(grad_act)
    grad_pre_low = grad_pre.astype(jnp.bfloat16)
    grad_ffn_bias = jnp.sum(grad_pre_low.astype(jnp.float32), axis=0)
    grad_ffn_in = jnp.einsum(
        "td,tf->df", normed_low, grad_pre_low, preferred_element_type=jnp.float32
    )
    hidden_part = jnp.einsum("tf,df->td", grad_pre_low, ffn_in, preferred_element_type=jnp.float32)
    grad_normed = grad_res_two + lax.psum(hidden_part, "tensor")
    grad_res_one, grad_gain_one, grad_shift_one = first_pull(grad_normed)
    att_low = grad_res_one.astype(jnp.bfloat16)
    grad_att_bias = jnp.sum(att_low.astype(jnp.float32), axis=0)
    grad_attn_out = jnp.einsum("te,td->ed", context, att_low, preferred_element_type=jnp.float32)
    grad_context = jnp.einsum(
        "td,ed->te", att_low, attn_out, preferred_element_type=jnp.float32
    ).astype(jnp.bfloat16)
    grad_query, grad_key, grad_value, scores_grad = lax.map(
        partial(attend_back, scale),
        (
            query_heads,
            key_heads,
            value_heads,
            prev_scores,
            segment_ids,
            row_lse,
            split_heads(grad_context),
        ),
    )
    grad_proj = jnp.stack(
        [
            grad_query.reshape(token_count, -1),
            grad_key.reshape(token_count, -1),
            grad_value.reshape(token_count, -1),
        ]
    )
    grad_attn_in = jnp.einsum("td,cte->cde", tokens, grad_proj, preferred_element_type=jnp.float32)
    grad_qv_bias = jnp.stack(
        [
            jnp.sum(grad_proj[0].astype(jnp.float32), axis=0),
            jnp.sum(grad_proj[2].astype(jnp.float32), axis=0),
        ]
    )
    input_part = jnp.einsum("cte,cde->td", grad_proj, attn_in, preferred_element_type=jnp.float32)
    norm_stack = jnp.stack([grad_gain_one, grad_gain_two, grad_shift_one, grad_shift_two])
    tokens_grad = grad_res_one + lax.psum(input_part, "tensor")
    grad_rows = jnp.stack(
        [
            norm_stack[0],
            norm_stack[1],
            grad_att_bias,
            norm_stack[2],
            grad_ffn_out_bias,
            norm_stack[3],
        ]
    )
    summed = lax.psum(
        (
            grad_attn_in,
            grad_attn_out,
            grad_ffn_in,
            grad_ffn_out,
            grad_qv_bias,
            grad_ffn_bias,
            grad_rows,
        ),
        "dp",
    )
    dp_index = lax.axis_index("dp")

    def own_part(whole_grad, shard, along):
        extent = shard.shape[along]
        return lax.dynamic_slice_in_dim(whole_grad, dp_index * extent, extent, along)

    shares = (
        own_part(summed[0], attn_in_master, 1),
        own_part(summed[1], attn_out_master, 1),
        own_part(summed[2], ffn_in_master, 0),
        own_part(summed[3], ffn_out_master, 1),
    )
    small_sums = (summed[4], summed[5], summed[6])
    local_squares = jnp.float32(0.0)
    for share in shares:
        local_squares = local_squares + jnp.sum(share * share)
    local_squares = (
        local_squares
        + (jnp.sum(small_sums[0] * small_sums[0]) + jnp.sum(small_sums[1] * small_sums[1]))
        / dp_count
    )
    local_squares = local_squares + jnp.sum(small_sums[2] * small_sums[2]) / (
        dp_count * tensor_count
    )
    total_squares = lax.psum(local_squares, ("dp", "tensor"))
    grad_norm = jnp.sqrt(total_squares)
    factor = 1.0 / jnp.maximum(grad_norm, 1.0)
    olds = (
        attn_in_master,
        attn_out_master,
        ffn_in_master,
        ffn_out_master,
        qv_bias,
        ffn_bias,
        row_params,
    )
    firsts = (
        attn_in_first,
        attn_out_first,
        ffn_in_first,
        ffn_out_first,
        qv_bias_first,
        ffn_bias_first,
        row_params_first,
    )
    seconds = (
        attn_in_second,
        attn_out_second,
        ffn_in_second,
        ffn_out_second,
        qv_bias_second,
        ffn_bias_second,
        row_params_second,
    )
    gradients = (
        shares[0],
        shares[1],
        shares[2],
        shares[3],
        small_sums[0],
        small_sums[1],
        small_sums[2],
    )
    decays = (weight_decay, weight_decay, weight_decay, weight_decay, 0.0, 0.0, 0.0)
    big_rate = D ** (-0.5)
    rates = (big_rate, big_rate, big_rate, big_rate, small_rate, small_rate, small_rate)
    updated = [
        adam_update(
            olds[place],
            gradients[place] * factor,
            firsts[place],
            seconds[place],
            decays[place],
            rates[place],
        )
        for place in range(7)
    ]
    return (
        final_low,
        tokens_grad,
        scores_grad,
        grad_norm,
        updated[0][0],
        updated[1][0],
        updated[2][0],
        updated[3][0],
        updated[0][1],
        updated[1][1],
        updated[2][1],
        updated[3][1],
        updated[0][2],
        updated[1][2],
        updated[2][2],
        updated[3][2],
        updated[0][0].astype(jnp.bfloat16),
        updated[1][0].astype(jnp.bfloat16),
        updated[2][0].astype(jnp.bfloat16),
        updated[3][0].astype(jnp.bfloat16),
        updated[4][0],
        updated[5][0],
        updated[6][0],
        updated[4][1],
        updated[5][1],
        updated[6][1],
        updated[4][2],
        updated[5][2],
        updated[6][2],
    )


def solution(mesh):
    in_specs = (
        P("dp", None),
        P("dp", None),
        P("dp", "tensor", None, None),
        P("dp", None),
        P(None, "dp", "tensor"),
        P("tensor", "dp"),
        P("dp", "tensor"),
        P("tensor", "dp"),
        P(None, "dp", "tensor"),
        P("tensor", "dp"),
        P("dp", "tensor"),
        P("tensor", "dp"),
        P(None, "dp", "tensor"),
        P("tensor", "dp"),
        P("dp", "tensor"),
        P("tensor", "dp"),
        P(None, "tensor"),
        P("tensor"),
        P(),
        P(None, "tensor"),
        P("tensor"),
        P(),
        P(None, "tensor"),
        P("tensor"),
        P(),
    )
    out_specs = (
        P("dp", None),
        P("dp", None),
        P("dp", "tensor", None, None),
        P(),
        P(None, "dp", "tensor"),
        P("tensor", "dp"),
        P("dp", "tensor"),
        P("tensor", "dp"),
        P(None, "dp", "tensor"),
        P("tensor", "dp"),
        P("dp", "tensor"),
        P("tensor", "dp"),
        P(None, "dp", "tensor"),
        P("tensor", "dp"),
        P("dp", "tensor"),
        P("tensor", "dp"),
        P(None, "dp", "tensor"),
        P("tensor", "dp"),
        P("dp", "tensor"),
        P("tensor", "dp"),
        P(None, "tensor"),
        P("tensor"),
        P(),
        P(None, "tensor"),
        P("tensor"),
        P(),
        P(None, "tensor"),
        P("tensor"),
        P(),
    )
    return jax.shard_map(
        on_device, mesh=mesh, in_specs=in_specs, out_specs=out_specs, check_vma=False
    )
```

profile of v0, /device:TPU:0, one launch (start us, length us, event | category | flops | bytes accessed | tf_op | source)
XLA Modules:
  0.0 938.5 jit_solution(11996233657050409264)
XLA Ops:
  9.2 38.6 %all_gather.12 = bf16[3,768,192]{2,0,1:T(4,128)(2,1)S(1)} all-gather(bf16[3,96,192]{2,0,1:T(4,128)(2,1)S(1)} %copy.141), channel_id=1, replica_groups=mesh['dp'=8,'tensor'=4] {'dp'}, dimensions={1}, use_global_device_ids=true | all-gather | bytes 995328 | tf_op jit(solution)/shard_map/all_gather | solution.py:108
  47.8 4.4 convolution_bitcast_fusion.1
  60.5 6.6 copy.146
  67.2 14.8 %while.28 = (s32[]{:T(128)}, bf16[3,512,3,64]{1,3,2,0:T(8,128)(2,1)S(1)}, f32[3,3,512,1]{2,1,3,0:T(4,128)S(1)}, bf16[3,512,3,64]{1,3,2,0:T(8,128)(2,1)}, s32[3,5...) while((s32[]{:T(128)}, ...), condition=%wide.region_3.4_spmd, body=%wide.region_0.3_spmd.sunk | while | flops 209549824 | bytes 12388973 | solution.py:131
  82.7 31.0 %all_gather.13 = bf16[192,768]{0,1:T(8,128)(2,1)S(1)} all-gather(bf16[192,96]{0,1:T(8,128)(2,1)S(1)} %copy.148), channel_id=1, replica_groups=mesh['dp'=8,'tensor'=4] {'dp'}, dimensions={1}, use_global_device_ids=true | all-gather | bytes 331776 | tf_op jit(solution)/shard_map/all_gather | solution.py:109
  113.7 3.0 fusion.98
  120.5 89.9 %all-reduce.8.cloned.1.call-done = f32[1536,768]{1,0:T(8,128)} async-done(((f32[1536,768]{1,0:T(8,128)}), f32[1536,768]{1,0:T(8,128)}) %all-reduce.8.cloned.1.call-update) | async-done | bytes 4718608 | tf_op jit(solution)/shard_map/psum | solution.py:138
  210.4 3.0 fusion.95
  216.7 14.5 %multiply_convert_fusion.2 = (bf16[1536,768]{1,0:T(8,128)(2,1)}, f32[1536,768]{1,0:T(8,128)}, f32[1536,768]{1,0:T(8,128)}) fusion(f32[768]{0:T(1024)S(1)} %copy-done.28, bf16[1536,768]{1,0:T(8,128)(2,1)S(1)} %fusion.62, bf16[768,768]{1,0:T(8,128)(2,1)} %all-gather.3.cloned.1.call-done), kind=kOutput, calls=%fused_computation.82 | convolution fusion | flops 1889796096 | bytes 15338496 | tf_op jit(solution)/shard_map/dot_general | solution.py:143
  231.2 6.2 fusion.99
  237.7 94.0 %all-reduce.10.cloned.1.call-done = f32[1536,768]{1,0:T(8,128)} async-done(((f32[1536,768]{1,0:T(8,128)}), f32[1536,768]{1,0:T(8,128)}) %all-reduce.10.cloned.1.call-update) | async-done | bytes 4718608 | tf_op jit(solution)/shard_map/psum | solution.py:147
  331.7 4.7 fusion.93
  340.4 3.8 fusion.92
  347.0 3.4 convert_reduce_fusion.2
  351.8 4.2 fusion.100
  356.1 5.3 fusion.102
  361.4 3.6 fusion.103
  365.0 85.4 %all-reduce.12.cloned.1.call-done = f32[1536,768]{1,0:T(8,128)} async-done(((f32[1536,768]{1,0:T(8,128)}), f32[1536,768]{1,0:T(8,128)}) %all-reduce.12.cloned.1.call-update) | async-done | bytes 4718608 | tf_op jit(solution)/shard_map/psum | solution.py:168
  450.3 6.7 multiply_reduce_fusion.2
  457.1 3.8 fusion.91
  468.6 55.0 %while.29 = (s32[]{:T(128)}, bf16[3,512,3,64]{1,3,2,0:T(8,128)(2,1)}, bf16[3,512,3,64]{1,3,2,0:T(8,128)(2,1)}, bf16[3,512,3,64]{1,3,2,0:T(8,128)(2,1)}, f32[3,3,...) while((s32[]{:T(128)}, ...), condition=%wide.region_17.18_spmd, body=%wide.region_15.17_spmd.sunk | while | flops 513505792 | bytes 43427472 | solution.py:176
  470.5 3.0 multiply_reduce_fusion.15
  488.8 3.0 multiply_reduce_fusion.15
  491.8 2.6 bitcast_convert_fusion.2
  507.1 3.0 multiply_reduce_fusion.15
  533.6 4.9 fusion.66
  540.5 4.5 convolution_bitcast_fusion
  548.2 39.3 %all-reduce = (f32[2,192]{1,0:T(2,128)S(1)}, f32[768]{0:T(1024)S(1)}, f32[6,768]{1,0:T(8,128)S(1)}) all-reduce(f32[2,192]{1,0:T(2,128)S(1)} %pad_maximum_fusion, f32[768]{0:T(1024)S(1)} %get-tuple-element.431, f32[6,768]{1,0:T(8,128)S(1)} %stack.31), channel_id=1, replica_groups=mesh['dp'=8,'tensor'=4] {'dp'}, use_global_device_ids=true, to_apply=%region_29.30 | all-reduce | flops 5760 | bytes 46080 | tf_op jit(solution)/shard_map/psum | solution.py:215
  591.2 183.0 %all-reduce.16.cloned.1.call-done = (f32[3,768,192]{1,2,0:T(8,128)}, f32[192,768]{1,0:T(8,128)}, f32[768,768]{1,0:T(8,128)}, f32[768,768]{0,1:T(8,128)}) async-done(((f32[3,768,192]{1,2,0:T(8,128)}, f32[192,768]{1,0:T(8,128)}, f32[768,768]{1,0:T(8,128)}, f32[768,768]{0,1:T(8,128)}), (f32[3,768,192]{1,2,0:T(8,128)}, f32[192,768]{1,0:T(8,128)}, f32[768,768]{1,0:T(8,128)}, ...) | async-done | bytes 7077904 | tf_op jit(solution)/shard_map/psum | solution.py:215
  783.6 86.5 %all-reduce.14.cloned.1.call-done = f32[1536,768]{1,0:T(8,128)} async-done(((f32[1536,768]{1,0:T(8,128)}), f32[1536,768]{1,0:T(8,128)}) %all-reduce.14.cloned.1.call-update) | async-done | bytes 4718608 | tf_op jit(solution)/shard_map/psum | solution.py:204
  870.1 6.5 add_add_fusion.4
  876.6 39.5 %psum.95 = f32[]{:T(128)} all-reduce(f32[]{:T(128)S(6)} %add.314), channel_id=1, replica_groups=mesh['dp'=8,'tensor'=4] {'dp','tensor'}, use_global_device_ids=true, to_apply=%region_42.43 | all-reduce | flops 1 | bytes 8 | tf_op jit(solution)/shard_map/psum | solution.py:251
  (233 shorter events, 127.3 us)
Async XLA Ops:
  8.0 202.4 %all-reduce.8.cloned.1.call-start = ((), (), s32[]{:S(2)}) async-start(), calls=%async_computation | async-start | bytes 9437184 | tf_op jit(solution)/shard_map/psum | solution.py:138
  60.5 6.7 copy-start.21
  67.2 15.5 %copy-start.13 = (f32[192,96]{1,0:T(8,128)S(1)}, f32[192,96]{1,0:T(8,128)}, u32[]{:S(2)}) copy-start(f32[192,96]{1,0:T(8,128)} %param.34) | copy-start | bytes 221188
  113.7 6.7 copy-start.22
  113.7 96.7 %copy-start.5 = (bf16[1536,768]{1,0:T(8,128)(2,1)S(1)}, bf16[1536,768]{1,0:T(8,128)(2,1)}, u32[]{:S(2)}) copy-start(bf16[1536,768]{1,0:T(8,128)(2,1)} %param.29) | copy-start | bytes 7077892
  116.8 99.9 %all-gather.3.cloned.1.call-start = ((), (), s32[]{:S(2)}) async-start(), calls=%async_computation.1 | async-start | bytes 1327104 | tf_op jit(solution)/shard_map/all_gather | solution.py:110
  118.5 112.7 %all-gather.5.cloned.1.call-start = ((), (), s32[]{:S(2)}) async-start(), calls=%async_computation.2 | async-start | bytes 1327104 | tf_op jit(solution)/shard_map/all_gather | solution.py:111
  120.2 211.5 %all-reduce.10.cloned.1.call-start = ((), (), s32[]{:S(2)}) async-start(), calls=%async_computation.3 | async-start | bytes 9437184 | tf_op jit(solution)/shard_map/psum | solution.py:147
  237.4 213.0 %all-reduce.12.cloned.1.call-start = ((), (), s32[]{:S(2)}) async-start(), calls=%async_computation.4 | async-start | bytes 9437184 | tf_op jit(solution)/shard_map/psum | solution.py:168
  340.3 6.5 slice-start
  340.3 6.5 slice-start.2
  340.4 6.5 slice-start.1
  340.4 6.5 slice-start.3
  346.9 4.8 copy-start.33
  356.0 418.2 %all-reduce.16.cloned.1.call-start = ((), (), s32[]{:S(2)}) async-start(), calls=%async_computation.6 | async-start | bytes 14155776 | tf_op jit(solution)/shard_map/psum | solution.py:215
  356.1 5.3 copy-start.7
  356.1 5.3 copy-start.35
  538.6 331.5 %all-reduce.14.cloned.1.call-start = ((), (), s32[]{:S(2)}) async-start(), calls=%async_computation.5 | async-start | bytes 9437184 | tf_op jit(solution)/shard_map/psum | solution.py:204
  783.6 138.2 %copy-start.14 = (f32[192,96]{1,0:T(8,128)S(1)}, f32[192,96]{1,0:T(8,128)}, u32[]{:S(2)}) copy-start(f32[192,96]{1,0:T(8,128)} %param.34) | copy-start | bytes 221188
  876.6 47.1 %copy-start.11 = (f32[96,768]{1,0:T(8,128)S(1)}, f32[96,768]{1,0:T(8,128)}, u32[]{:S(2)}) copy-start(f32[96,768]{1,0:T(8,128)} %param.35) | copy-start | bytes 884740
  876.6 47.1 %copy-start.17 = (f32[96,768]{1,0:T(8,128)S(1)}, f32[96,768]{1,0:T(8,128)}, u32[]{:S(2)}) copy-start(f32[96,768]{1,0:T(8,128)} %param.39) | copy-start | bytes 884740
  876.6 47.1 %copy-start.18 = (f32[96,768]{1,0:T(8,128)S(1)}, f32[96,768]{1,0:T(8,128)}, u32[]{:S(2)}) copy-start(f32[96,768]{1,0:T(8,128)} %param.43) | copy-start | bytes 884740
  876.6 49.2 %copy-start.12 = (f32[768,96]{0,1:T(8,128)S(1)}, f32[768,96]{0,1:T(8,128)}, u32[]{:S(2)}) copy-start(f32[768,96]{0,1:T(8,128)} %param.36) | copy-start | bytes 884740
  876.6 49.2 %copy-start.19 = (f32[768,96]{0,1:T(8,128)S(1)}, f32[768,96]{0,1:T(8,128)}, u32[]{:S(2)}) copy-start(f32[768,96]{0,1:T(8,128)} %param.40) | copy-start | bytes 884740
  916.9 11.1 %copy-start.27 = (f32[2,192]{1,0:T(2,128)S(1)}, f32[2,192]{1,0:T(2,128)}, u32[]{:S(2)}) copy-start(f32[2,192]{1,0:T(2,128)} %param.45) | copy-start | bytes 4612
  916.9 12.3 %copy-start.23 = (f32[6,768]{1,0:T(8,128)S(1)}, f32[6,768]{1,0:T(8,128)}, u32[]{:S(2)}) copy-start(f32[6,768]{1,0:T(8,128)} %param.47) | copy-start | bytes 55300
  918.3 9.6 %copy-start.31 = (f32[2,192]{1,0:T(2,128)S(1)}, f32[2,192]{1,0:T(2,128)}, u32[]{:S(2)}) copy-start(f32[2,192]{1,0:T(2,128)} %param.48) | copy-start | bytes 4612
  918.3 9.6 %copy-start.32 = (f32[2,192]{1,0:T(2,128)S(1)}, f32[2,192]{1,0:T(2,128)}, u32[]{:S(2)}) copy-start(f32[2,192]{1,0:T(2,128)} %param.51) | copy-start | bytes 4612
  918.3 10.2 %copy-start.29 = (f32[768]{0:T(1024)S(1)}, f32[768]{0:T(1024)}, u32[]{:S(2)}) copy-start(f32[768]{0:T(1024)} %param.49) | copy-start | bytes 9220
  918.3 10.2 %copy-start.30 = (f32[768]{0:T(1024)S(1)}, f32[768]{0:T(1024)}, u32[]{:S(2)}) copy-start(f32[768]{0:T(1024)} %param.52) | copy-start | bytes 9220
  918.3 10.8 %copy-start.24 = (f32[6,768]{1,0:T(8,128)S(1)}, f32[6,768]{1,0:T(8,128)}, u32[]{:S(2)}) copy-start(f32[6,768]{1,0:T(8,128)} %param.50) | copy-start | bytes 55300
  918.3 10.8 %copy-start.25 = (f32[6,768]{1,0:T(8,128)S(1)}, f32[6,768]{1,0:T(8,128)}, u32[]{:S(2)}) copy-start(f32[6,768]{1,0:T(8,128)} %param.53) | copy-start | bytes 55300
  (15 other events, 32.5 us)
Sparse Core Ops, SparseCore 0:
  116.9 93.4 all-reduce.7
  237.5 94.1 all-reduce.9
  356.1 94.1 all-reduce.11
Sparse Core Ops, SparseCore 1:
  120.0 40.8 all-gather.2
  163.5 39.9 all-gather.4
  538.6 235.5 all-reduce.15
  777.3 92.7 all-reduce.13
where the time goes:
time: 947 us; the launch traced here: 938 us
  waiting for transfers between devices  539 us (57%)
  blocking collectives  148 us (16%)
  matrix products  102 us (11%)
  other arithmetic  69.2 us (7%)
  local copies, waits for them, and re-layouts  56 us (6%)
  between operations  22.9 us (2%)
    psum x1, waiting for transfers between devices, on_device(): lax.psum((grad_attn_in, grad_attn_out, grad_ffn_in, grad_ffn_out, grad_qv...  183 us
    psum x1, waiting for transfers between devices, on_device(): ffn_output = lax.psum(ffn_partial, 'tensor') + row_params[4]  94 us
    psum x1, waiting for transfers between devices, on_device(): attended = lax.psum(attn_partial, 'tensor') + row_params[2]  89.9 us
    psum x1, waiting for transfers between devices, on_device(): tokens_grad = grad_res_one + lax.psum(input_part, 'tensor')  86.5 us
    psum x1, waiting for transfers between devices, on_device(): grad_normed = grad_res_two + lax.psum(hidden_part, 'tensor')  85.4 us
    psum x1, blocking collectives, on_device(): total_squares = lax.psum(local_squares, ('dp', 'tensor'))  39.5 us
    psum x1, blocking collectives, on_device(): lax.psum((grad_attn_in, grad_attn_out, grad_ffn_in, grad_ffn_out, grad_qv...  39.3 us
    all_gather x1, blocking collectives, on_device(): lax.all_gather(attn_in_master.astype(jnp.bfloat16), 'dp', axis=1, tiled=T...  38.6 us
  transfers between devices with their start and end apart: 7, of which 5 were waited for; matrix products, arithmetic and copies ran while one was open for 5% of the time, Pallas kernels for 0%

commit v1 on v0

--- a/solution.py
+++ b/solution.py
@@ -12,6 +12,12 @@
 adam_eps = 1e-08
 norm_eps = 1e-06
 small_rate = 0.5
+
+
+def summed_here(shard, name):
+    blocks = lax.all_gather(shard, name, axis=0, tiled=False)
+    result = blocks.sum(axis=0)
+    return result
 
 
 def layer_norm(rows_in, gain_row, shift_row):
@@ -201,7 +207,7 @@
     )
     input_part = jnp.einsum("cte,cde->td", grad_proj, attn_in, preferred_element_type=jnp.float32)
     norm_stack = jnp.stack([grad_gain_one, grad_gain_two, grad_shift_one, grad_shift_two])
-    tokens_grad = grad_res_one + lax.psum(input_part, "tensor")
+    tokens_grad = grad_res_one + summed_here(input_part, "tensor")
     grad_rows = jnp.stack(
         [
             norm_stack[0],

time: 947 us -> 859 us (0.907)
  waiting for transfers between devices: 539 us -> 454 us
  matrix products: 102 us -> 88.7 us
  other arithmetic: 69.2 us -> 81.5 us
    psum x1 -> x0, waiting for transfers between devices: 86.5 us -> none  [on_device(): tokens_grad = grad_res_one + lax.psum(input_part, 'tensor')]
    reduce_sum x0 -> x1, other arithmetic: none -> 10.4 us  [summed_here(): result = blocks.sum(axis=0)]
  transfers between devices with their start and end apart: 7 -> 7, of which waited for: 5 -> 4; matrix products, arithmetic and copies ran while one was open for 5% -> 7% of each run, Pallas kernels for 0% -> 0%
where the time goes in v1:
time: 859 us; the launch traced here: 851 us
  waiting for transfers between devices  454 us (53%)
  blocking collectives  150 us (17%)
  matrix products  88.7 us (10%)
  other arithmetic  81.5 us (9%)
  local copies, waits for them, and re-layouts  53.4 us (6%)
  between operations  22.9 us (3%)
    psum x1, waiting for transfers between devices, on_device(): lax.psum((grad_attn_in, grad_attn_out, grad_ffn_in, grad_ffn_out, grad_qv...  183 us
    psum x1, waiting for transfers between devices, on_device(): ffn_output = lax.psum(ffn_partial, 'tensor') + row_params[4]  94 us
    psum x1, waiting for transfers between devices, on_device(): attended = lax.psum(attn_partial, 'tensor') + row_params[2]  91.7 us
    psum x1, waiting for transfers between devices, on_device(): grad_normed = grad_res_two + lax.psum(hidden_part, 'tensor')  84.5 us
    psum x1, blocking collectives, on_device(): lax.psum((grad_attn_in, grad_attn_out, grad_ffn_in, grad_ffn_out, grad_qv...  39.4 us
    psum x1, blocking collectives, on_device(): total_squares = lax.psum(local_squares, ('dp', 'tensor'))  39 us
    all_gather x1, blocking collectives, on_device(): lax.all_gather(attn_in_master.astype(jnp.bfloat16), 'dp', axis=1, tiled=T...  38.6 us
    all_gather x1, blocking collectives, on_device(): lax.all_gather(attn_out_master.astype(jnp.bfloat16), 'dp', axis=1, tiled=...  33 us
  transfers between devices with their start and end apart: 7, of which 4 were waited for; matrix products, arithmetic and copies ran while one was open for 7% of the time, Pallas kernels for 0%

profile of v1, /device:TPU:0, one launch (start us, length us, event | category | flops | bytes accessed | tf_op | source)
XLA Modules:
  0.0 851.1 jit_solution(1842483922507633566)
XLA Ops:
  9.2 38.6 %all_gather.18 = bf16[3,768,192]{2,0,1:T(4,128)(2,1)S(1)} all-gather(bf16[3,96,192]{2,0,1:T(4,128)(2,1)S(1)} %copy.141), channel_id=1, replica_groups=mesh['dp'=8,'tensor'=4] {'dp'}, dimensions={1}, use_global_device_ids=true | all-gather | bytes 995328 | tf_op jit(solution)/shard_map/all_gather | solution.py:114
  47.8 4.4 convolution_bitcast_fusion.1
  53.7 33.0 %all_gather.19 = bf16[192,768]{0,1:T(8,128)(2,1)} all-gather(bf16[192,96]{0,1:T(8,128)(2,1)S(1)} %copy.148), channel_id=1, replica_groups=mesh['dp'=8,'tensor'=4] {'dp'}, dimensions={1}, use_global_device_ids=true | all-gather | bytes 331776 | tf_op jit(solution)/shard_map/all_gather | solution.py:115
  91.2 6.6 copy.146
  97.9 11.3 %while.28 = (s32[]{:T(128)}, bf16[3,512,3,64]{1,3,2,0:T(8,128)(2,1)S(1)}, f32[3,3,512,1]{2,1,3,0:T(4,128)S(1)}, bf16[3,512,3,64]{1,3,2,0:T(8,128)(2,1)S(1)}, s32...) while((s32[]{:T(128)}, ...), condition=%wide.region_3.4_spmd, body=%wide.region_0.3_spmd.sunk | while | flops 209549824 | bytes 12388973 | solution.py:137
  110.0 3.0 fusion.98
  114.8 91.7 %all-reduce.7.cloned.1.call-done = f32[1536,768]{1,0:T(8,128)} async-done(((f32[1536,768]{1,0:T(8,128)}), f32[1536,768]{1,0:T(8,128)}) %all-reduce.7.cloned.1.call-update) | async-done | bytes 4718608 | tf_op jit(solution)/shard_map/psum | solution.py:144
  206.5 3.8 fusion.95
  214.5 15.1 %multiply_convert_fusion.2 = (bf16[1536,768]{1,0:T(8,128)(2,1)}, f32[1536,768]{1,0:T(8,128)}, f32[1536,768]{1,0:T(8,128)}) fusion(f32[768]{0:T(1024)S(1)} %copy-done.33, bf16[1536,768]{1,0:T(8,128)(2,1)} %fusion.62, bf16[768,768]{1,0:T(8,128)(2,1)} %all-gather.5.cloned.1.call-done), kind=kOutput, calls=%fused_computation.82 | convolution fusion | flops 1889796096 | bytes 15338496 | tf_op jit(solution)/shard_map/dot_general | solution.py:149
  229.6 6.2 fusion.99
  236.1 94.0 %all-reduce.9.cloned.1.call-done = f32[1536,768]{1,0:T(8,128)} async-done(((f32[1536,768]{1,0:T(8,128)}), f32[1536,768]{1,0:T(8,128)}) %all-reduce.9.cloned.1.call-update) | async-done | bytes 4718608 | tf_op jit(solution)/shard_map/psum | solution.py:153
  330.1 4.7 fusion.93
  338.8 3.8 fusion.92
  345.4 4.0 convert_reduce_fusion.2
  350.9 4.2 fusion.100
  355.2 6.1 fusion.102
  361.3 3.6 fusion.103
  364.9 84.5 %all-reduce.11.cloned.1.call-done = f32[1536,768]{1,0:T(8,128)} async-done(((f32[1536,768]{1,0:T(8,128)}), f32[1536,768]{1,0:T(8,128)}) %all-reduce.11.cloned.1.call-update) | async-done | bytes 4718608 | tf_op jit(solution)/shard_map/psum | solution.py:174
  449.4 6.7 multiply_reduce_fusion.2
  456.2 3.8 fusion.91
  466.5 46.8 %while.29 = (s32[]{:T(128)}, bf16[3,512,3,64]{1,3,2,0:T(8,128)(2,1)}, bf16[3,512,3,64]{1,3,2,0:T(8,128)(2,1)}, bf16[3,512,3,64]{1,3,2,0:T(8,128)(2,1)}, f32[3,3,...) while((s32[]{:T(128)}, ...), condition=%wide.region_17.18_spmd, body=%wide.region_15.17_spmd.sunk | while | flops 513505792 | bytes 60731108 | solution.py:182
  467.4 2.8 multiply_reduce_fusion.15
  474.2 3.6 copy.204
  489.9 3.6 copy.204
  505.4 3.6 copy.204
  521.1 4.4 fusion.66
  527.5 4.5 convolution_bitcast_fusion
  534.9 39.4 %all-reduce = (f32[2,192]{1,0:T(2,128)S(1)}, f32[768]{0:T(1024)S(1)}, f32[6,768]{1,0:T(8,128)S(1)}) all-reduce(f32[2,192]{1,0:T(2,128)S(1)} %pad_maximum_fusion, f32[768]{0:T(1024)S(1)} %copy-done.34, f32[6,768]{1,0:T(8,128)S(1)} %stack.31), channel_id=1, replica_groups=mesh['dp'=8,'tensor'=4] {'dp'}, use_global_device_ids=true, to_apply=%region_29.30 | all-reduce | flops 5760 | bytes 46080 | tf_op jit(solution)/shard_map/psum | solution.py:221
  578.0 183.3 %all-reduce.13.cloned.1.call-done = (f32[3,768,192]{1,2,0:T(8,128)}, f32[192,768]{1,0:T(8,128)}, f32[768,768]{1,0:T(8,128)}, f32[768,768]{0,1:T(8,128)}) async-done(((f32[3,768,192]{1,2,0:T(8,128)}, f32[192,768]{1,0:T(8,128)}, f32[768,768]{1,0:T(8,128)}, f32[768,768]{0,1:T(8,128)}), (f32[3,768,192]{1,2,0:T(8,128)}, f32[192,768]{1,0:T(8,128)}, f32[768,768]{1,0:T(8,128)}, ...) | async-done | bytes 7077904 | tf_op jit(solution)/shard_map/psum | solution.py:221
  770.8 39.0 %psum.87 = f32[]{:T(128)} all-reduce(f32[]{:T(128)S(6)} %add.312), channel_id=1, replica_groups=mesh['dp'=8,'tensor'=4] {'dp','tensor'}, use_global_device_ids=true, to_apply=%region_42.43 | all-reduce | flops 1 | bytes 8 | tf_op jit(solution)/shard_map/psum | solution.py:257
  825.6 10.4 %reduce_sum.283 = f32[1536,768]{1,0:T(8,128)} reduce(f32[4,1536,768]{2,1,0:T(8,128)} %bitcast.171, f32[]{:T(128)} %constant.74.clone.1), dimensions={0}, to_apply=%region_18.19 | reduce | flops 3538944 | bytes 23592964 | tf_op jit(solution)/shard_map/reduce_sum | solution.py:19
  836.0 6.5 add_add_fusion.4
  (250 shorter events, 109.0 us)
Async XLA Ops:
  8.0 198.5 %all-reduce.7.cloned.1.call-start = ((), (), s32[]{:S(2)}) async-start(), calls=%async_computation | async-start | bytes 9437184 | tf_op jit(solution)/shard_map/psum | solution.py:144
  47.8 4.4 copy-start.13
  91.2 6.7 copy-start.29
  97.9 12.0 %copy-start.8 = (bf16[192,768]{0,1:T(8,128)(2,1)S(1)}, bf16[192,768]{0,1:T(8,128)(2,1)}, u32[]{:S(2)}) copy-start(bf16[192,768]{0,1:T(8,128)(2,1)} %all_gather.19) | copy-start | bytes 884740
  109.9 3.9 copy-start.16
  110.0 4.8 copy-start.30
  113.0 101.5 %all-gather.5.cloned.1.call-start = ((), (), s32[]{:S(2)}) async-start(), calls=%async_computation.1 | async-start | bytes 1327104 | tf_op jit(solution)/shard_map/all_gather | solution.py:116
  113.8 115.8 %all-gather.7.cloned.1.call-start = ((), (), s32[]{:S(2)}) async-start(), calls=%async_computation.2 | async-start | bytes 1327104 | tf_op jit(solution)/shard_map/all_gather | solution.py:117
  114.5 215.6 %all-reduce.9.cloned.1.call-start = ((), (), s32[]{:S(2)}) async-start(), calls=%async_computation.3 | async-start | bytes 9437184 | tf_op jit(solution)/shard_map/psum | solution.py:153
  235.8 213.6 %all-reduce.11.cloned.1.call-start = ((), (), s32[]{:S(2)}) async-start(), calls=%async_computation.4 | async-start | bytes 9437184 | tf_op jit(solution)/shard_map/psum | solution.py:174
  338.7 6.5 slice-start
  338.7 6.5 slice-start.2
  338.8 6.5 slice-start.1
  338.8 6.5 slice-start.3
  345.3 4.0 copy-start.11
  345.3 5.5 copy-start.35
  355.1 406.2 %all-reduce.13.cloned.1.call-start = ((), (), s32[]{:S(2)}) async-start(), calls=%async_computation.6 | async-start | bytes 14155776 | tf_op jit(solution)/shard_map/psum | solution.py:221
  355.2 6.1 copy-start.12
  355.2 6.1 copy-start.37
  466.5 3.7 copy-start.6
  482.1 3.7 copy-start.6
  497.7 3.7 copy-start.6
  513.3 4.9 copy-start.10
  525.6 300.0 %all-gather.9.cloned.1.call-start = ((), (), s32[]{:S(2)}) async-start(), calls=%async_computation.5 | async-start | bytes 23592960 | tf_op jit(solution)/shard_map/all_gather | solution.py:18
  532.0 238.6 %copy-start.23 = (f32[3,96,192]{2,1,0:T(8,128)S(1)}, f32[3,96,192]{2,1,0:T(8,128)}, u32[]{:S(2)}) copy-start(f32[3,96,192]{2,1,0:T(8,128)} %param.41) | copy-start | bytes 663556
  532.0 286.0 %copy-start.31 = (f32[6,768]{1,0:T(8,128)S(1)}, f32[6,768]{1,0:T(8,128)}, u32[]{:S(2)}) copy-start(f32[6,768]{1,0:T(8,128)} %param.47) | copy-start | bytes 55300
  532.0 287.4 %copy-start.21 = (f32[192,96]{1,0:T(8,128)S(1)}, f32[192,96]{1,0:T(8,128)}, u32[]{:S(2)}) copy-start(f32[192,96]{1,0:T(8,128)} %param.34) | copy-start | bytes 221188
  532.1 289.3 %copy-start.17 = (f32[768,96]{0,1:T(8,128)S(1)}, f32[768,96]{0,1:T(8,128)}, u32[]{:S(2)}) copy-start(f32[768,96]{0,1:T(8,128)} %param.36) | copy-start | bytes 884740
  532.1 289.3 %copy-start.24 = (f32[768,96]{0,1:T(8,128)S(1)}, f32[768,96]{0,1:T(8,128)}, u32[]{:S(2)}) copy-start(f32[768,96]{0,1:T(8,128)} %param.40) | copy-start | bytes 884740
  532.1 289.2 %copy-start.25 = (f32[768,96]{0,1:T(8,128)S(1)}, f32[768,96]{0,1:T(8,128)}, u32[]{:S(2)}) copy-start(f32[768,96]{0,1:T(8,128)} %param.44) | copy-start | bytes 884740
  534.6 288.8 %copy-start.19 = (f32[96,768]{1,0:T(8,128)S(1)}, f32[96,768]{1,0:T(8,128)}, u32[]{:S(2)}) copy-start(f32[96,768]{1,0:T(8,128)} %param.35) | copy-start | bytes 884740
  534.7 288.8 %copy-start.26 = (f32[96,768]{1,0:T(8,128)S(1)}, f32[96,768]{1,0:T(8,128)}, u32[]{:S(2)}) copy-start(f32[96,768]{1,0:T(8,128)} %param.39) | copy-start | bytes 884740
  (23 other events, 45.8 us)
Sparse Core Ops, SparseCore 0:
  113.1 93.3 all-reduce.6
  235.9 94.1 all-reduce.8
  355.2 94.1 all-reduce.10
  532.1 120.0 all-gather.8
Sparse Core Ops, SparseCore 1:
  116.3 40.8 all-gather.4
  159.8 39.9 all-gather.6
  525.7 235.6 all-reduce.12
